TPU v7x, 256 devices: a whole 4x4x8 slice. The times are simulated.
256 devices in a mesh: row: 32 (over z, y), col: 8 (over x, core).
Axes of the slice: x: 4, y: 4, z: 8, core: 2. Of those that a mesh axis runs over, the one named last changes fastest.
Arguments:
- edit_keys: bfloat16 [256, 14336], P('row', 'col'), may hold values from -6.75 to 6.75
- edit_shifts: bfloat16 [256, 4096], P('row', 'col'), may hold values from -6 to 6
- ridge_scale: float32 [1], replicated, may hold values from 0.5 to 2
Outputs:
- panel_a: float32 [14336, 256], P('row')
- panel_b: float32 [14336, 256], P('row')
- trailing: float32 [14336, 14336], P('row', 'col')
- forward: float32 [14336, 4096], P('row', 'col')
All inputs are finite; a program needn't handle non-finite values.
Results may differ from a plain program's by a relative error of at most 0.0003.
Values may be sent and summed in bfloat16 or wider, within the bound.
A program may use at most 64 MiB of HBM per device.

v0:
```python
import functools

import jax
import jax.numpy as jnp
from jax import lax
from jax.experimental import pallas as pl
from jax.experimental.pallas import tpu as pltpu
from jax.sharding import PartitionSpec as P

F32, BF16 = jnp.float32, jnp.bfloat16
PANEL = 256
ROWS, COLS, YS = 32, 8, 4
ZS = ROWS // YS
SLAB = 8
UNITS = 14336
COL_UNITS = UNITS // COLS
ROW_UNITS = UNITS // ROWS
SHIFTS = 512
WIDE = COL_UNITS + SHIFTS
WIN = 512
KEYS = 256
MESH = pl.DeviceIdType.MESH


def split2(x):
    high = x.astype(BF16)
    return high, (x - high.astype(F32)).astype(BF16)


def split3(x):
    high = x.astype(BF16)
    rest = x - high.astype(F32)
    mid = rest.astype(BF16)
    return high, mid, (rest - mid.astype(F32)).astype(BF16)


def mm(a, b):
    return jnp.dot(a, b, preferred_element_type=F32)


def mm_nt(a, b):
    return lax.dot_general(a, b, (((1,), (1,)), ((), ())), preferred_element_type=F32)


def remote(src, dst, send, recv, row, col):
    return pltpu.make_async_remote_copy(
        src_ref=src, dst_ref=dst, send_sem=send, recv_sem=recv, device_id=(row, col), device_id_type=MESH
    )


def window_start(y):
    return y * ROW_UNITS - 64 * lax.rem(y, 2)


def exchange_kernel(
    keys, shifts, crit, sums, wide, window, own_sum, col_sums,
    s_local, s_send1, r_sum1, r_crit1, s_send2, r_sum2, r_crit2, s_y, r_y, s_z, r_z, s_w, r_w,
):
    row, col = lax.axis_index("row"), lax.axis_index("col")
    z, y = row // YS, lax.rem(row, YS)

    barrier = pltpu.get_barrier_semaphore()

    def greet_row(i, carry):
        pl.semaphore_signal(barrier, inc=1, device_id=(lax.rem(row + i, ROWS), col), device_id_type=MESH)
        return carry

    def greet_col(i, carry):
        pl.semaphore_signal(barrier, inc=1, device_id=(row, lax.rem(col + i, COLS)), device_id_type=MESH)
        return carry

    lax.fori_loop(1, COLS, greet_col, 0)
    lax.fori_loop(1, ROWS, greet_row, 0)

    k32 = keys[...].astype(F32)
    sq = k32 * k32
    part = sq[:, 0:128]
    for t in range(1, COL_UNITS // 128):
        part = part + sq[:, 128 * t : 128 * (t + 1)]
    own_sum[0] = jnp.sum(part, axis=0, keepdims=True)

    local = [
        pltpu.make_async_copy(keys, wide.at[row, :, pl.ds(0, COL_UNITS)], s_local.at[0]),
        pltpu.make_async_copy(shifts, wide.at[row, :, pl.ds(COL_UNITS, SHIFTS)], s_local.at[1]),
        pltpu.make_async_copy(own_sum.at[0], col_sums.at[col], s_local.at[2]),
    ]
    for copy in local:
        copy.start()

    for half in range(2):

        @pl.when(col == half)
        def _():
            copy = pltpu.make_async_copy(
                keys.at[:, pl.ds(0, PANEL)], crit.at[row, :, pl.ds(half * PANEL, PANEL)], s_local.at[3]
            )
            copy.start()
            copy.wait()

    @pl.when(z == col)
    def _():
        for yy in range(YS):
            start = yy * ROW_UNITS - 64 * (yy % 2)

            @pl.when(y == yy)
            def _():
                copy = pltpu.make_async_copy(keys.at[:, pl.ds(start, WIN)], window.at[row], s_local.at[3])
                copy.start()
                copy.wait()

    pl.semaphore_wait(barrier, ROWS + COLS - 2)

    def send_sum1(i, carry):
        remote(own_sum.at[0], col_sums.at[col], s_send1.at[0], r_sum1, row, lax.rem(col + i, COLS)).start()
        return carry

    for half in range(2):

        @pl.when(col == half)
        def _():
            def send_crit1(i, carry):
                remote(
                    keys.at[:, pl.ds(0, PANEL)],
                    crit.at[row, :, pl.ds(half * PANEL, PANEL)],
                    s_send1.at[1],
                    r_crit1.at[half],
                    row,
                    lax.rem(col + i, COLS),
                ).start()
                return carry

            lax.fori_loop(1, COLS, send_crit1, 0)

    lax.fori_loop(1, COLS, send_sum1, 0)
    for copy in local:
        copy.wait()
    pltpu.make_async_copy(col_sums.at[pl.ds(0, COLS - 1)], col_sums.at[pl.ds(0, COLS - 1)], r_sum1).wait()
    for half in range(2):

        @pl.when(col != half)
        def _():
            ref = crit.at[row, :, pl.ds(half * PANEL, PANEL)]
            pltpu.make_async_copy(ref, ref, r_crit1.at[half]).wait()

    def send2(i, carry):
        peer = lax.rem(row + i, ROWS)
        remote(crit.at[row], crit.at[row], s_send2.at[0], r_crit2, peer, col).start()
        remote(col_sums, sums.at[row], s_send2.at[1], r_sum2, peer, col).start()
        return carry

    lax.fori_loop(1, ROWS, send2, 0)
    copy = pltpu.make_async_copy(col_sums, sums.at[row], s_local.at[3])
    copy.start()
    copy.wait()

    def await_bytes(ref, sem):
        pltpu.make_async_copy(ref, ref, sem).wait()

    await_bytes(crit.at[pl.ds(0, ROWS - 1)], r_crit2)
    await_bytes(sums.at[pl.ds(0, ROWS - 1)], r_sum2)

    def send_y(i, carry):
        peer = z * YS + lax.rem(y + i, YS)
        remote(wide.at[row], wide.at[row], s_y, r_y, peer, col).start()
        return carry

    lax.fori_loop(1, YS, send_y, 0)

    def send_window(yy):
        start = yy * ROW_UNITS - 64 * (yy % 2)
        target = col * YS + yy

        def body(i, carry):
            @pl.when((target != row) | (i != col))
            def _():
                remote(keys.at[:, pl.ds(start, WIN)], window.at[row], s_w, r_w, target, i).start()

            return carry

        lax.fori_loop(0, COLS, body, 0)

    for yy in range(YS):
        send_window(yy)

    await_bytes(wide.at[pl.ds(0, YS - 1)], r_y)

    up = lax.rem(z + 1, ZS) * YS + y
    down = lax.rem(z + ZS - 1, ZS) * YS + y
    for step in range(4):
        from_below = lax.rem(z + ZS - step, ZS) * YS
        from_above = lax.rem(z + step, ZS) * YS
        count = YS if step < 3 else YS // 2
        ref = wide.at[pl.ds(from_below, count)]
        remote(ref, ref, s_z.at[0, step], r_z.at[0, step], up, col).start()
        ref = wide.at[pl.ds(from_above + YS - count, count)]
        remote(ref, ref, s_z.at[1, step], r_z.at[1, step], down, col).start()
        await_bytes(wide.at[pl.ds(0, count)], r_z.at[0, step])
        await_bytes(wide.at[pl.ds(0, count)], r_z.at[1, step])

    @pl.when(z == col)
    def _():
        await_bytes(window.at[pl.ds(0, ROWS - 1)], r_w)

    @pl.when(z != col)
    def _():
        await_bytes(window, r_w)

    await_bytes(col_sums.at[pl.ds(0, COLS - 1)], s_send1.at[0])

    @pl.when(col < 2)
    def _():
        await_bytes(crit.at[pl.ds(0, COLS - 1), :, pl.ds(0, PANEL)], s_send1.at[1])

    await_bytes(crit.at[pl.ds(0, ROWS - 1)], s_send2.at[0])
    await_bytes(sums.at[pl.ds(0, ROWS - 1)], s_send2.at[1])
    await_bytes(wide.at[pl.ds(0, YS - 1)], s_y)

    @pl.when(row // YS == col)
    def _():
        await_bytes(window.at[pl.ds(0, ROWS - 1)], s_w)

    @pl.when(row // YS != col)
    def _():
        await_bytes(window, s_w)

    for step in range(4):
        count = YS if step < 3 else YS // 2
        for way in range(2):
            await_bytes(wide.at[pl.ds(0, count)], s_z.at[way, step])


def exchange(keys, shifts):
    dma = pltpu.SemaphoreType.DMA
    vmem = pl.BlockSpec(memory_space=pltpu.VMEM)
    return pl.pallas_call(
        exchange_kernel,
        out_shape=(
            jax.ShapeDtypeStruct((ROWS, SLAB, 2 * PANEL), BF16),
            jax.ShapeDtypeStruct((ROWS, COLS, 1, 128), F32),
            jax.ShapeDtypeStruct((ROWS, SLAB, WIDE), BF16),
            jax.ShapeDtypeStruct((ROWS, SLAB, WIN), BF16),
        ),
        in_specs=[vmem, vmem],
        out_specs=(vmem, vmem, vmem, vmem),
        scratch_shapes=[
            pltpu.VMEM((1, 1, 128), F32),
            pltpu.VMEM((COLS, 1, 128), F32),
            dma((4,)), dma((2,)), dma, dma((2,)), dma((2,)), dma, dma, dma, dma, dma((2, 4)), dma((2, 4)), dma, dma,
        ],
        compiler_params=pltpu.CompilerParams(collective_id=0, has_side_effects=True),
        name="exchange",
    )(keys, shifts)


def row_bcast(v, k):
    return jnp.broadcast_to(v[k : k + 1, :], (8, v.shape[1]))


def factor16(R, base, s, j, nt, diag_next):
    o = 16 * j
    iota = lax.broadcasted_iota(jnp.int32, (8, 128), 0)
    last = j == 7
    ng = 2 if last else 4
    lanes = slice(128 * s, 128 * s + 128)
    T = list(diag_next) if diag_next is not None else [R[base + 8 * g : base + 8 * g + 8, lanes] for g in range(2)]
    for g in range(2, ng):
        T.append(R[base + 8 * g : base + 8 * g + 8, lanes])
    C = [[None] * 4 for _ in range(16)]
    for k in range(16):
        for g in range(k // 8, ng):
            C[k][g] = jnp.broadcast_to(T[g][:, o + k : o + k + 1], (8, 128))
    Y = {t: [R[base + 8 * g : base + 8 * g + 8, 128 * t : 128 * t + 128] for g in range(2)] for t in range(s + 1, nt)}
    rv = [jnp.zeros((8, 128), F32)] * 2
    for k in range(16):
        gk, kk = k // 8, k % 8
        p = row_bcast(C[k][gk], kk)
        rp = 1.0 / p
        rv[gk] = jnp.where(iota == kk, lax.rsqrt(p), rv[gk])
        M = [None] * 4
        for g in range(gk, ng):
            M[g] = C[k][g] * rp
        for jj in range(k + 1, 16):
            c = row_bcast(C[k][jj // 8], jj % 8)
            for g in range(jj // 8, ng):
                C[jj][g] = C[jj][g] - M[g] * c
        M[gk] = None if kk == 7 else jnp.where(iota > kk, M[gk], 0.0)
        yk = row_bcast(T[gk], kk)
        for g in range(gk, ng):
            if M[g] is not None:
                T[g] = T[g] - M[g] * yk
        for t in range(s + 1, nt):
            yk = row_bcast(Y[t][gk], kk)
            for g in range(gk, 2):
                if M[g] is not None:
                    Y[t][g] = Y[t][g] - M[g] * yk
    U = {s: jnp.concatenate([T[0] * rv[0], T[1] * rv[1]], axis=0)}
    for t in range(s + 1, nt):
        U[t] = jnp.concatenate([Y[t][0] * rv[0], Y[t][1] * rv[1]], axis=0)
    for t in range(s, nt):
        R[base : base + 16, 128 * t : 128 * t + 128] = U[t]
    if last:
        return None
    zero = jnp.zeros((16, 128), BF16)
    parts = {t: split3(U[t]) for t in range(s, nt)}
    h, m, l = parts[s]
    left = jnp.concatenate([h, h, m, h, l, m, zero, zero], axis=0)
    left = jnp.transpose(left.astype(F32)).astype(BF16)[16 * (j + 1) :, :]
    below = 16 * (7 - j)
    for t in range(s, nt):
        h, m, l = parts[t]
        right = jnp.concatenate([h, m, h, l, h, m, zero, zero], axis=0)
        if t == s:
            if below > 16:
                R[base + 32 : base + 16 + below, lanes] -= mm(left[16:], right)
        else:
            R[base + 16 : base + 16 + below, 128 * t : 128 * t + 128] -= mm(left, right)
    return T[2], T[3]


def factor_kernel(ridge, kp_ref, sums_ref, u_ref, m_ref, amount_ref):
    nsuper = 4
    n = 2 * PANEL
    nt = nsuper + 2
    R = u_ref
    total = jnp.sum(jnp.sum(sums_ref[...], axis=0, keepdims=True), axis=1, keepdims=True)
    amount = ridge[0] * total / UNITS
    amount_ref[...] = jnp.broadcast_to(amount, (8, 128))
    kp = kp_ref[...]
    kpt = jnp.transpose(kp.astype(F32))
    R[:, n:] = kpt
    kptb = kpt.astype(BF16)
    i0 = lax.broadcasted_iota(jnp.int32, (128, 128), 0)
    i1 = lax.broadcasted_iota(jnp.int32, (128, 128), 1)
    for s in range(nsuper):
        rows = slice(128 * s, 128 * s + 128)
        R[rows, 128 * s : n] = mm(kptb[rows, :], kp[:, 128 * s :])
        R[rows, rows] += jnp.where(i0 == i1, jnp.broadcast_to(amount, (128, 128)), 0.0)
    i0 = lax.broadcasted_iota(jnp.int32, (KEYS, KEYS), 0)
    i1 = lax.broadcasted_iota(jnp.int32, (KEYS, KEYS), 1)
    m_ref[...] = jnp.where(i0 == i1, 1.0, 0.0).astype(F32)
    for s in range(nsuper):
        following = None
        for j in range(8):
            following = factor16(R, 128 * s + 16 * j, s, j, nt, following)
        us = R[128 * s : 128 * s + 128, 128 * s + 128 :]
        h, m, l = split3(us)
        right = [jnp.concatenate([h, m], 0), jnp.concatenate([h, l], 0), jnp.concatenate([h, m], 0)]
        for t in range(s + 1, nt):
            c0 = 128 * (t - s - 1)
            lh, lm, ll = split3(jnp.transpose(us[:, c0 : c0 + 128]))
            left = [jnp.concatenate([lh, lh], 1), jnp.concatenate([lm, lh], 1), jnp.concatenate([ll, lm], 1)]
            update = (
                mm(left[0], right[0][:, c0:]) + mm(left[1], right[1][:, c0:]) + mm(left[2], right[2][:, c0:])
            )
            if t < nsuper:
                R[128 * t : 128 * t + 128, 128 * t :] -= update
            else:
                q = 128 * (t - nsuper)
                m_ref[q : q + 128, q:] -= update
    m_ref[128:, :128] = jnp.transpose(m_ref[:128, 128:])


def factor(ridge, kp, sums):
    vmem = pl.BlockSpec(memory_space=pltpu.VMEM)
    return pl.pallas_call(
        factor_kernel,
        out_shape=(
            jax.ShapeDtypeStruct((2 * PANEL, 2 * PANEL + KEYS), F32),
            jax.ShapeDtypeStruct((KEYS, KEYS), F32),
            jax.ShapeDtypeStruct((8, 128), F32),
        ),
        in_specs=[pl.BlockSpec(memory_space=pltpu.SMEM), vmem, vmem],
        out_specs=(vmem, vmem, vmem),
        name="factor",
    )(ridge, kp, sums)


def output_kernel(
    u_ref, m_ref, amount_ref, win_ref, wide_ref, pa_out, pb_out, tr_out, fw_out,
    kt, pa, pb, tr, fw, sems,
):
    row, col = lax.axis_index("row"), lax.axis_index("col")
    z, y = row // YS, lax.rem(row, YS)
    kt[...] = jnp.transpose(win_ref[...].astype(F32)).astype(BF16)
    off = pl.multiple_of(64 * lax.rem(y, 2), 64)
    k_rows = kt[pl.ds(off, ROW_UNITS), :]
    qt = u_ref[:, 2 * PANEL :]
    qh, ql = split2(qt)
    q2 = jnp.concatenate([qh, ql], axis=1)
    both = mm_nt(jnp.concatenate([k_rows, k_rows], axis=1), q2)
    pa[...] = both[:, :PANEL]
    pb[...] = both[:, PANEL:]
    i0 = lax.broadcasted_iota(jnp.int32, (PANEL, PANEL), 0)
    i1 = lax.broadcasted_iota(jnp.int32, (PANEL, PANEL), 1)

    @pl.when(row == 0)
    def _():
        pa[:PANEL, :] = jnp.where(i0 >= i1, jnp.transpose(u_ref[:PANEL, :PANEL]), 0.0)
        pb[:PANEL, :] = jnp.zeros((PANEL, PANEL), F32)

    @pl.when(row == YS)
    def _():
        pb[:PANEL, :] = jnp.where(i0 >= i1, jnp.transpose(u_ref[PANEL : 2 * PANEL, PANEL : 2 * PANEL]), 0.0)

    copies = [pltpu.make_async_copy(pa, pa_out, sems.at[0]), pltpu.make_async_copy(pb, pb_out, sems.at[1])]
    for copy in copies:
        copy.start()

    mh, mm_, ml = split3(m_ref[...])
    t = mm(jnp.concatenate([k_rows, k_rows, k_rows], axis=1), jnp.concatenate([mh, mm_, ml], axis=0))
    th, tl = split2(t)
    t2 = jnp.concatenate([th, tl], axis=1)

    v = wide_ref[:, COL_UNITS:]
    v2 = jnp.concatenate([v, v], axis=0)
    fw[...] = mm(t2, v2)

    @pl.when(row == 0)
    def _():
        fw[:PANEL, :] = mm(q2[:PANEL], v2)

    @pl.when(row == YS)
    def _():
        fw[:PANEL, :] = mm(q2[PANEL:], v2)

    copies.append(pltpu.make_async_copy(fw, fw_out, sems.at[2]))
    copies[-1].start()

    for q in range(COL_UNITS // 256):
        lanes = pl.ds(256 * q, 256)
        k = wide_ref[:, 256 * q : 256 * q + 256]
        tr[:, lanes] = mm(t2, jnp.concatenate([k, k], axis=0))

        @pl.when(z == col)
        def _():
            r0 = lax.broadcasted_iota(jnp.int32, (ROW_UNITS, 256), 0)
            r1 = lax.broadcasted_iota(jnp.int32, (ROW_UNITS, 256), 1)
            hit = r1 + (256 * q) == r0 + y * ROW_UNITS
            tr[:, lanes] += jnp.where(hit, amount_ref[0:1, 0:1], 0.0)

        @pl.when((row == 0) | (row == YS))
        def _():
            tr[:PANEL, lanes] = jnp.zeros((PANEL, 256), F32)

        if q == 0:

            @pl.when(col < 2)
            def _():
                tr[:, lanes] = jnp.zeros((ROW_UNITS, 256), F32)

        copies.append(pltpu.make_async_copy(tr.at[:, lanes], tr_out.at[:, lanes], sems.at[3 + q]))
        copies[-1].start()
    for copy in copies:
        copy.wait()


def outputs(u, m, amount, win, wide):
    vmem = pl.BlockSpec(memory_space=pltpu.VMEM)
    anyspace = pl.BlockSpec(memory_space=pl.ANY)
    shapes = [(ROW_UNITS, PANEL), (ROW_UNITS, PANEL), (ROW_UNITS, COL_UNITS), (ROW_UNITS, SHIFTS)]
    return pl.pallas_call(
        output_kernel,
        out_shape=tuple(jax.ShapeDtypeStruct(s, F32) for s in shapes),
        in_specs=[vmem] * 5,
        out_specs=(anyspace,) * 4,
        scratch_shapes=[pltpu.VMEM((WIN, KEYS), BF16)]
        + [pltpu.VMEM(s, F32) for s in shapes]
        + [pltpu.SemaphoreType.DMA((3 + COL_UNITS // 256,))],
        name="outputs",
    )(u, m, amount, win, wide)


def on_device(edit_keys, edit_shifts, ridge_scale):
    crit, sums, wide, window = exchange(edit_keys, edit_shifts)
    kp = crit.reshape(KEYS, 2 * PANEL)
    u, m, amount = factor(ridge_scale, kp, sums.reshape(ROWS * COLS, 128))
    return outputs(u, m, amount, window.reshape(KEYS, WIN), wide.reshape(KEYS, WIDE))


def solution(mesh):
    return jax.shard_map(
        on_device,
        mesh=mesh,
        in_specs=(P("row", "col"), P("row", "col"), P()),
        out_specs=(P("row", None), P("row", None), P("row", "col"), P("row", "col")),
        check_vma=False,
    )
```

profile of v0, /device:TPU:1, one launch (start us, length us, event | category | flops | bytes accessed | tf_op | source)
XLA Modules:
  0.0 84.4 jit_solution(54037659043284330)
XLA Ops:
  1.3 60.9 %exchange.1 = (bf16[32,8,512]{2,1,0:T(8,128)(2,1)}, f32[32,8,1,128]{3,2,1,0:T(1,128)}, bf16[32,8,2304]{2,1,0:T(8,128)(2,1)}, bf16[32,8,512]{2,1,0:T(8,128)(2,1)}) custom-call(bf16[8,1792]{1,0:T(8,128)(2,1)} %keys.1, bf16[8,512]{1,0:T(8,128)(2,1)} %shifts.1), custom_call_target="tpu_custom_call" | custom-call | tf_op jit(solution)/shard_map/exchange/pallas_call | solution.py:235
  62.2 14.5 %factor.1 = (f32[512,768]{1,0:T(8,128)}, f32[256,256]{1,0:T(8,128)}, f32[8,128]{1,0:T(8,128)}) custom-call(f32[1]{0:T(128)S(6)} %copy.7.ridge, bf16[256,512]{1,0:T(8,128)(2,1)} %bitcast.6, f32[256,128]{1,0:T(8,128)} %bitcast.7), custom_call_target="tpu_custom_call" | custom-call | tf_op jit(solution)/shard_map/factor/pallas_call | solution.py:365
  76.6 7.6 %outputs.1 = (f32[448,256]{1,0:T(8,128)}, f32[448,256]{1,0:T(8,128)}, f32[448,1792]{1,0:T(8,128)}, f32[448,512]{1,0:T(8,128)}) custom-call(f32[512,768]{1,0:T(8,128)} %get-tuple-element.13.u_ref, f32[256,256]{1,0:T(8,128)} %get-tuple-element.14.m_ref, f32[8,128]{1,0:T(8,128)} %get-tuple-element.15.amount_ref, bf16[256,512]{1,0:T(8,128)(2,1)} %bitcast.5, ...), custom_call_target="tpu_custom_call" | custom-call | tf_op jit(solution)/shard_map/outputs/pallas_call | solution.py:461
where the time goes:
time: 86.1 us; the launch traced here: 84.4 us
  Pallas kernels  83 us (96%)
  between operations  1.45 us (2%)
    pallas_call x1, Pallas kernels, exchange(): pl.pallas_call(exchange_kernel, out_shape=(jax.ShapeDtypeStruct((ROWS, SL...  60.9 us
    pallas_call x1, Pallas kernels, factor(): pl.pallas_call(factor_kernel, out_shape=(jax.ShapeDtypeStruct((2 * PANEL,...  14.5 us
    pallas_call x1, Pallas kernels, outputs(): pl.pallas_call(output_kernel, out_shape=tuple((jax.ShapeDtypeStruct(s, F3...  7.64 us

commit v1 on v0

v1 whole, which is shorter than its diff:
```python
import functools

import jax
import jax.numpy as jnp
from jax import lax
from jax.experimental import pallas as pl
from jax.experimental.pallas import tpu as pltpu
from jax.sharding import PartitionSpec as P

F32, BF16 = jnp.float32, jnp.bfloat16
PANEL = 256
ROWS, COLS, YS = 32, 8, 4
ZS = ROWS // YS
SLAB = 8
UNITS = 14336
COL_UNITS = UNITS // COLS
ROW_UNITS = UNITS // ROWS
SHIFTS = 512
WIDE = COL_UNITS + SHIFTS
WIN = 512
KEYS = 256
MESH = pl.DeviceIdType.MESH


def split2(x):
    high = x.astype(BF16)
    return high, (x - high.astype(F32)).astype(BF16)


def split3(x):
    high = x.astype(BF16)
    rest = x - high.astype(F32)
    mid = rest.astype(BF16)
    return high, mid, (rest - mid.astype(F32)).astype(BF16)


def mm(a, b):
    return jnp.dot(a, b, preferred_element_type=F32)


def mm_nt(a, b):
    return lax.dot_general(a, b, (((1,), (1,)), ((), ())), preferred_element_type=F32)


def remote(src, dst, send, recv, row, col):
    return pltpu.make_async_remote_copy(
        src_ref=src, dst_ref=dst, send_sem=send, recv_sem=recv, device_id=(row, col), device_id_type=MESH
    )


def row_bcast(v, k):
    return jnp.broadcast_to(v[k : k + 1, :], (8, v.shape[1]))


def factor16(R, base, s, j, nt, diag_next):
    o = 16 * j
    iota = lax.broadcasted_iota(jnp.int32, (8, 128), 0)
    last = j == 7
    ng = 2 if last else 4
    lanes = slice(128 * s, 128 * s + 128)
    T = list(diag_next) if diag_next is not None else [R[base + 8 * g : base + 8 * g + 8, lanes] for g in range(2)]
    for g in range(2, ng):
        T.append(R[base + 8 * g : base + 8 * g + 8, lanes])
    C = [[None] * 4 for _ in range(16)]
    for k in range(16):
        for g in range(k // 8, ng):
            C[k][g] = jnp.broadcast_to(T[g][:, o + k : o + k + 1], (8, 128))
    Y = {t: [R[base + 8 * g : base + 8 * g + 8, 128 * t : 128 * t + 128] for g in range(2)] for t in range(s + 1, nt)}
    rv = [jnp.zeros((8, 128), F32)] * 2
    for k in range(16):
        gk, kk = k // 8, k % 8
        p = row_bcast(C[k][gk], kk)
        rp = 1.0 / p
        rv[gk] = jnp.where(iota == kk, lax.rsqrt(p), rv[gk])
        M = [None] * 4
        for g in range(gk, ng):
            M[g] = C[k][g] * rp
        for jj in range(k + 1, 16):
            c = row_bcast(C[k][jj // 8], jj % 8)
            for g in range(jj // 8, ng):
                C[jj][g] = C[jj][g] - M[g] * c
        M[gk] = None if kk == 7 else jnp.where(iota > kk, M[gk], 0.0)
        yk = row_bcast(T[gk], kk)
        for g in range(gk, ng):
            if M[g] is not None:
                T[g] = T[g] - M[g] * yk
        for t in range(s + 1, nt):
            yk = row_bcast(Y[t][gk], kk)
            for g in range(gk, 2):
                if M[g] is not None:
                    Y[t][g] = Y[t][g] - M[g] * yk
    U = {s: jnp.concatenate([T[0] * rv[0], T[1] * rv[1]], axis=0)}
    for t in range(s + 1, nt):
        U[t] = jnp.concatenate([Y[t][0] * rv[0], Y[t][1] * rv[1]], axis=0)
    for t in range(s, nt):
        R[base : base + 16, 128 * t : 128 * t + 128] = U[t]
    if last:
        return None
    zero = jnp.zeros((16, 128), BF16)
    parts = {t: split3(U[t]) for t in range(s, nt)}
    h, m, l = parts[s]
    left = jnp.concatenate([h, h, m, h, l, m, zero, zero], axis=0)
    left = jnp.transpose(left.astype(F32)).astype(BF16)[16 * (j + 1) :, :]
    below = 16 * (7 - j)
    for t in range(s, nt):
        h, m, l = parts[t]
        right = jnp.concatenate([h, m, h, l, h, m, zero, zero], axis=0)
        if t == s:
            if below > 16:
                R[base + 32 : base + 16 + below, lanes] -= mm(left[16:], right)
        else:
            R[base + 16 : base + 16 + below, 128 * t : 128 * t + 128] -= mm(left, right)
    return T[2], T[3]


XS = COLS // 2
A_LANES = pl.ds(0, 1152)
B_LANES = pl.ds(1152, 1152)
B_HALVES = (pl.ds(1152, 640), pl.ds(1792, 512))


def fused_kernel(
    ridge, keys, shifts, wide, window, q2_out, m_ref, amount_ref, u_out,
    crit, sums, own_sum, x_sums, R,
    s_local, s_x, r_x, s_r, r_r, s_p, r_p, s_y, r_y, s_a, r_a, s_b, r_b, s_yb, r_yb, s_w, r_w, s_v, r_v,
):
    row, col = lax.axis_index("row"), lax.axis_index("col")
    z, y = row // YS, lax.rem(row, YS)
    x, core = col // 2, lax.rem(col, 2)
    partner = 2 * x + 1 - core

    def await_bytes(ref, sem):
        pltpu.make_async_copy(ref, ref, sem).wait()

    barrier = pltpu.get_barrier_semaphore()

    def greet(r, c):
        pl.semaphore_signal(barrier, inc=1, device_id=(r, c), device_id_type=MESH)

    def greet_row(i, carry):
        greet(lax.rem(row + i, ROWS), col)
        return carry

    for i in range(1, XS):
        greet(row, lax.rem(col + 2 * i, COLS))
    greet(row, partner)
    lax.fori_loop(1, ROWS, greet_row, 0)

    k32 = keys[...].astype(F32)
    sq = k32 * k32
    part = sq[:, 0:128]
    for t in range(1, COL_UNITS // 128):
        part = part + sq[:, 128 * t : 128 * (t + 1)]
    own_sum[0] = jnp.sum(part, axis=0, keepdims=True)

    local = [
        pltpu.make_async_copy(keys, wide.at[row, :, pl.ds(0, COL_UNITS)], s_local.at[0]),
        pltpu.make_async_copy(shifts, wide.at[row, :, pl.ds(COL_UNITS, SHIFTS)], s_local.at[1]),
    ]
    for copy in local:
        copy.start()

    @pl.when(col < 2)
    def _():
        copy = pltpu.make_async_copy(keys.at[:, pl.ds(0, PANEL)], crit.at[core, row], s_local.at[2])
        copy.start()
        copy.wait()

    @pl.when(z == col)
    def _():
        for yy in range(YS):
            start = yy * ROW_UNITS - 64 * (yy % 2)

            @pl.when(y == yy)
            def _():
                copy = pltpu.make_async_copy(keys.at[:, pl.ds(start, WIN)], window.at[row], s_local.at[2])
                copy.start()
                copy.wait()

    for copy in local:
        copy.wait()
    pl.semaphore_wait(barrier, ROWS + XS - 1)

    @pl.when(col < 2)
    def _():
        for i in range(1, XS):
            remote(
                keys.at[:, pl.ds(0, PANEL)], crit.at[core, row], s_x.at[0], r_x.at[0], row, lax.rem(col + 2 * i, COLS)
            ).start()

    for i in range(1, XS):
        remote(own_sum.at[0], x_sums.at[x], s_x.at[1], r_x.at[1], row, lax.rem(col + 2 * i, COLS)).start()
    x_sums[x] = own_sum[0]

    @pl.when(col >= 2)
    def _():
        await_bytes(crit.at[0, 0], r_x.at[0])

    def send_slab(i, carry):
        remote(crit.at[core, row], crit.at[core, row], s_r.at[0], r_r.at[0], lax.rem(row + i, ROWS), col).start()
        return carry

    def send_sum(i, carry):
        remote(sums.at[core, row], sums.at[core, row], s_r.at[1], r_r.at[1], lax.rem(row + i, ROWS), col).start()
        return carry

    await_bytes(x_sums.at[pl.ds(0, XS - 1)], r_x.at[1])
    sums[core, row] = jnp.sum(x_sums[...], axis=0)
    lax.fori_loop(1, ROWS, send_slab, 0)
    lax.fori_loop(1, ROWS, send_sum, 0)
    await_bytes(crit.at[0, pl.ds(0, ROWS - 1)], r_r.at[0])
    await_bytes(sums.at[0, pl.ds(0, ROWS - 1)], r_r.at[1])

    remote(crit.at[core], crit.at[core], s_p.at[0], r_p.at[0], row, partner).start()
    remote(sums.at[core], sums.at[core], s_p.at[1], r_p.at[1], row, partner).start()

    up = lax.rem(z + 1, ZS) * YS
    down = lax.rem(z + ZS - 1, ZS) * YS

    def over_y(slot, lanes, send, recv):
        for i in range(1, YS):
            ref = wide.at[slot * YS + y, :, lanes]
            remote(ref, ref, send, recv, z * YS + lax.rem(y + i, YS), col).start()

    def round_b(step):
        for way, (source, target) in enumerate(((lax.rem(z + ZS - step, ZS), up), (lax.rem(z + step, ZS), down))):
            lanes = B_LANES if step < 3 else B_HALVES[way]
            ref = wide.at[source * YS + y, :, lanes]
            remote(ref, ref, s_b.at[way, step], r_b.at[way, step], target + y, col).start()

    def wait_b(step, sems):
        for way in range(2):
            lanes = B_LANES if step < 3 else B_HALVES[way]
            await_bytes(wide.at[0, :, lanes], sems.at[way, step])

    def pairs_a(step, way):
        return (0, 1) if step < 3 else (way,)

    def round_a(step):
        for pair in range(2):
            for way, (source, target) in enumerate(((lax.rem(z + ZS - step, ZS), up), (lax.rem(z + step, ZS), down))):
                if step > 0:
                    await_bytes(wide.at[pl.ds(0, 2), :, A_LANES], r_a.at[way, step - 1, pair])
                if pair in pairs_a(step, way):
                    ref = wide.at[pl.ds(source * YS + 2 * pair, 2), :, A_LANES]
                    remote(ref, ref, s_a.at[way, step, pair], r_a.at[way, step, pair], target + y, col).start()

    def b_over_y(step):
        if step < 3:
            over_y(lax.rem(z + ZS - step - 1, ZS), B_LANES, s_yb.at[0, step], r_yb.at[0, step])
            over_y(lax.rem(z + step + 1, ZS), B_LANES, s_yb.at[1, step], r_yb.at[1, step])
        else:
            over_y(lax.rem(z + ZS // 2, ZS), B_LANES, s_yb.at[0, step], r_yb.at[0, step])

    over_y(z, pl.ds(0, WIDE), s_y, r_y)
    round_b(0)

    for yy in range(YS):
        start = yy * ROW_UNITS - 64 * (yy % 2)
        target = col * YS + yy
        for i in range(XS):

            @pl.when((target != row) | (i != x))
            def _():
                remote(keys.at[:, pl.ds(start, WIN)], window.at[row], s_w, r_w, target, 2 * i + core).start()

    def swap_window():
        @pl.when(core == lax.rem(z, 2))
        def _():
            @pl.when(col == z)
            def _():
                await_bytes(window.at[pl.ds(0, ROWS - 1)], r_w)

            @pl.when(col != z)
            def _():
                await_bytes(window, r_w)

            remote(window, window, s_v, r_v, row, partner).start()

    def hook1():
        await_bytes(wide.at[pl.ds(0, YS - 1)], r_y)
        round_a(0)
        wait_b(0, r_b)
        round_b(1)
        b_over_y(0)

    def hook2():
        round_a(1)
        wait_b(1, r_b)
        round_b(2)
        b_over_y(1)

    def hook3():
        round_a(2)
        wait_b(2, r_b)
        round_b(3)
        b_over_y(2)

    def hook4():
        round_a(3)
        wait_b(3, r_b)
        b_over_y(3)

    hooks = {3: hook1, 9: hook2, 15: hook3, 21: hook4, 24: swap_window}

    await_bytes(crit.at[0], r_p.at[0])
    await_bytes(sums.at[0], r_p.at[1])

    nsuper = 4
    n = 2 * PANEL
    nt = nsuper + 2
    total = jnp.sum(sums[0] + sums[1], axis=0)
    total = jnp.sum(total, axis=1, keepdims=True)
    amount = ridge[0] * total / UNITS
    amount_ref[...] = jnp.broadcast_to(amount, (8, 128))
    first = crit[0].astype(F32).reshape(KEYS, PANEL)
    second = crit[1].astype(F32).reshape(KEYS, PANEL)
    kp32 = jnp.concatenate([first, second], axis=1)
    kp = kp32.astype(BF16)
    kpt = jnp.transpose(kp32)
    R[:, n:] = kpt
    kptb = kpt.astype(BF16)
    i0 = lax.broadcasted_iota(jnp.int32, (128, 128), 0)
    i1 = lax.broadcasted_iota(jnp.int32, (128, 128), 1)
    for s in range(nsuper):
        rows = slice(128 * s, 128 * s + 128)
        R[rows, 128 * s : n] = mm(kptb[rows, :], kp[:, 128 * s :])
        R[rows, rows] += jnp.where(i0 == i1, jnp.broadcast_to(amount, (128, 128)), 0.0)
    i0 = lax.broadcasted_iota(jnp.int32, (KEYS, KEYS), 0)
    i1 = lax.broadcasted_iota(jnp.int32, (KEYS, KEYS), 1)
    m_ref[...] = jnp.where(i0 == i1, 1.0, 0.0).astype(F32)
    for s in range(nsuper):
        following = None
        for j in range(8):
            following = factor16(R, 128 * s + 16 * j, s, j, nt, following)
            if 8 * s + j in hooks:
                hooks[8 * s + j]()
        us = R[128 * s : 128 * s + 128, 128 * s + 128 :]
        h, m, l = split3(us)
        right = [jnp.concatenate([h, m], 0), jnp.concatenate([h, l], 0), jnp.concatenate([h, m], 0)]
        for t in range(s + 1, nt):
            c0 = 128 * (t - s - 1)
            lh, lm, ll = split3(jnp.transpose(us[:, c0 : c0 + 128]))
            left = [jnp.concatenate([lh, lh], 1), jnp.concatenate([lm, lh], 1), jnp.concatenate([ll, lm], 1)]
            update = (
                mm(left[0], right[0][:, c0:]) + mm(left[1], right[1][:, c0:]) + mm(left[2], right[2][:, c0:])
            )
            if t < nsuper:
                R[128 * t : 128 * t + 128, 128 * t :] -= update
            else:
                q = 128 * (t - nsuper)
                m_ref[q : q + 128, q:] -= update
    m_ref[128:, :128] = jnp.transpose(m_ref[:128, 128:])
    qh, ql = split2(R[:, n:])
    q2_out[...] = jnp.concatenate([qh, ql], axis=1)

    for half in range(2):

        @pl.when(row == YS * half)
        def _():
            part = pl.ds(PANEL * half, PANEL)
            copy = pltpu.make_async_copy(R.at[part, part], u_out, s_local.at[2])
            copy.start()
            copy.wait()

    for way in range(2):
        for pair in pairs_a(3, way):
            await_bytes(wide.at[pl.ds(0, 2), :, A_LANES], r_a.at[way, 3, pair])
    for step in range(4):
        for way in range(2 if step < 3 else 1):
            await_bytes(wide.at[pl.ds(0, YS - 1), :, B_LANES], r_yb.at[way, step])

    @pl.when(core != lax.rem(z, 2))
    def _():
        await_bytes(window, r_v)

    @pl.when(col < 2)
    def _():
        await_bytes(crit.at[0, pl.ds(0, XS - 1)], s_x.at[0])

    await_bytes(x_sums.at[pl.ds(0, XS - 1)], s_x.at[1])
    await_bytes(crit.at[0, pl.ds(0, ROWS - 1)], s_r.at[0])
    await_bytes(sums.at[0, pl.ds(0, ROWS - 1)], s_r.at[1])
    await_bytes(crit.at[0], s_p.at[0])
    await_bytes(sums.at[0], s_p.at[1])
    await_bytes(wide.at[pl.ds(0, YS - 1)], s_y)
    for step in range(4):
        wait_b(step, s_b)
        for way in range(2):
            for pair in pairs_a(step, way):
                await_bytes(wide.at[pl.ds(0, 2), :, A_LANES], s_a.at[way, step, pair])
        for way in range(2 if step < 3 else 1):
            await_bytes(wide.at[pl.ds(0, YS - 1), :, B_LANES], s_yb.at[way, step])

    @pl.when(z == col)
    def _():
        await_bytes(window.at[pl.ds(0, YS * XS - 1)], s_w)

    @pl.when(z != col)
    def _():
        await_bytes(window.at[pl.ds(0, YS * XS)], s_w)

    @pl.when(core == lax.rem(z, 2))
    def _():
        await_bytes(window, s_v)


def fused(ridge, keys, shifts):
    dma = pltpu.SemaphoreType.DMA
    vmem = pl.BlockSpec(memory_space=pltpu.VMEM)
    anyspace = pl.BlockSpec(memory_space=pl.ANY)
    return pl.pallas_call(
        fused_kernel,
        out_shape=(
            jax.ShapeDtypeStruct((ROWS, SLAB, WIDE), BF16),
            jax.ShapeDtypeStruct((ROWS, SLAB, WIN), BF16),
            jax.ShapeDtypeStruct((2 * PANEL, 2 * KEYS), BF16),
            jax.ShapeDtypeStruct((KEYS, KEYS), F32),
            jax.ShapeDtypeStruct((8, 128), F32),
            jax.ShapeDtypeStruct((PANEL, PANEL), F32),
        ),
        in_specs=[pl.BlockSpec(memory_space=pltpu.SMEM), vmem, vmem],
        out_specs=(anyspace, anyspace, vmem, vmem, vmem, anyspace),
        scratch_shapes=[
            pltpu.VMEM((2, ROWS, SLAB, PANEL), BF16),
            pltpu.VMEM((2, ROWS, 1, 128), F32),
            pltpu.VMEM((1, 1, 128), F32),
            pltpu.VMEM((XS, 1, 128), F32),
            pltpu.VMEM((2 * PANEL, 2 * PANEL + KEYS), F32),
            dma((3,)), dma((2,)), dma((2,)), dma((2,)), dma((2,)), dma((2,)), dma((2,)), dma, dma,
            dma((2, 4, 2)), dma((2, 4, 2)), dma((2, 4)), dma((2, 4)), dma((2, 4)), dma((2, 4)),
            dma, dma, dma, dma,
        ],
        compiler_params=pltpu.CompilerParams(collective_id=0, has_side_effects=True),
        name="fused",
    )(ridge, keys, shifts)


def output_kernel(
    q2_ref, m_ref, amount_ref, u_ref, win_ref, wide_ref, pa_out, pb_out, tr_out, fw_out,
    kt, pa, pb, tr, fw, sems,
):
    row, col = lax.axis_index("row"), lax.axis_index("col")
    z, y = row // YS, lax.rem(row, YS)
    kt[...] = jnp.transpose(win_ref[...].astype(F32)).astype(BF16)
    off = pl.multiple_of(64 * lax.rem(y, 2), 64)
    k_rows = kt[pl.ds(off, ROW_UNITS), :]
    q2 = q2_ref[...]
    both = mm_nt(jnp.concatenate([k_rows, k_rows], axis=1), q2)
    pa[...] = both[:, :PANEL]
    pb[...] = both[:, PANEL:]
    i0 = lax.broadcasted_iota(jnp.int32, (PANEL, PANEL), 0)
    i1 = lax.broadcasted_iota(jnp.int32, (PANEL, PANEL), 1)

    @pl.when(row == 0)
    def _():
        pa[:PANEL, :] = jnp.where(i0 >= i1, jnp.transpose(u_ref[...]), 0.0)
        pb[:PANEL, :] = jnp.zeros((PANEL, PANEL), F32)

    @pl.when(row == YS)
    def _():
        pb[:PANEL, :] = jnp.where(i0 >= i1, jnp.transpose(u_ref[...]), 0.0)

    copies = [pltpu.make_async_copy(pa, pa_out, sems.at[0]), pltpu.make_async_copy(pb, pb_out, sems.at[1])]
    for copy in copies:
        copy.start()

    mh, mm_, ml = split3(m_ref[...])
    t = mm(jnp.concatenate([k_rows, k_rows, k_rows], axis=1), jnp.concatenate([mh, mm_, ml], axis=0))
    th, tl = split2(t)
    t2 = jnp.concatenate([th, tl], axis=1)

    v = wide_ref[:, COL_UNITS:]
    v2 = jnp.concatenate([v, v], axis=0)
    fw[...] = mm(t2, v2)

    @pl.when(row == 0)
    def _():
        fw[:PANEL, :] = mm(q2[:PANEL], v2)

    @pl.when(row == YS)
    def _():
        fw[:PANEL, :] = mm(q2[PANEL:], v2)

    copies.append(pltpu.make_async_copy(fw, fw_out, sems.at[2]))
    copies[-1].start()

    for q in range(COL_UNITS // 256):
        lanes = pl.ds(256 * q, 256)
        k = wide_ref[:, 256 * q : 256 * q + 256]
        tr[:, lanes] = mm(t2, jnp.concatenate([k, k], axis=0))

        @pl.when(z == col)
        def _():
            r0 = lax.broadcasted_iota(jnp.int32, (ROW_UNITS, 256), 0)
            r1 = lax.broadcasted_iota(jnp.int32, (ROW_UNITS, 256), 1)
            hit = r1 + (256 * q) == r0 + y * ROW_UNITS
            tr[:, lanes] += jnp.where(hit, amount_ref[0:1, 0:1], 0.0)

        @pl.when((row == 0) | (row == YS))
        def _():
            tr[:PANEL, lanes] = jnp.zeros((PANEL, 256), F32)

        if q == 0:

            @pl.when(col < 2)
            def _():
                tr[:, lanes] = jnp.zeros((ROW_UNITS, 256), F32)

        copies.append(pltpu.make_async_copy(tr.at[:, lanes], tr_out.at[:, lanes], sems.at[3 + q]))
        copies[-1].start()
    for copy in copies:
        copy.wait()


def outputs(q2, m, amount, u, win, wide):
    vmem = pl.BlockSpec(memory_space=pltpu.VMEM)
    anyspace = pl.BlockSpec(memory_space=pl.ANY)
    shapes = [(ROW_UNITS, PANEL), (ROW_UNITS, PANEL), (ROW_UNITS, COL_UNITS), (ROW_UNITS, SHIFTS)]
    return pl.pallas_call(
        output_kernel,
        out_shape=tuple(jax.ShapeDtypeStruct(s, F32) for s in shapes),
        in_specs=[vmem] * 6,
        out_specs=(anyspace,) * 4,
        scratch_shapes=[pltpu.VMEM((WIN, KEYS), BF16)]
        + [pltpu.VMEM(s, F32) for s in shapes]
        + [pltpu.SemaphoreType.DMA((3 + COL_UNITS // 256,))],
        name="outputs",
    )(q2, m, amount, u, win, wide)


def on_device(edit_keys, edit_shifts, ridge_scale):
    wide, window, q2, m, amount, u = fused(ridge_scale, edit_keys, edit_shifts)
    return outputs(q2, m, amount, u, window.reshape(KEYS, WIN), wide.reshape(KEYS, WIDE))


def solution(mesh):
    return jax.shard_map(
        on_device,
        mesh=mesh,
        in_specs=(P("row", "col"), P("row", "col"), P()),
        out_specs=(P("row", None), P("row", None), P("row", "col"), P("row", "col")),
        check_vma=False,
    )
```

time: 86.1 us -> 57.2 us (0.66); the launches traced: 84.4 us -> 57 us
  Pallas kernels: 83 us -> 55.6 us
    pallas_call x2 -> x1, Pallas kernels: 75.4 us -> 48.2 us  [fused(): pl.pallas_call(fused_kernel, out_shape=(jax.ShapeDtypeStruct((ROWS, SLAB,...]
where the time goes in v1:
time: 57.2 us; the launch traced here: 57 us
  Pallas kernels  55.6 us (97%)
  between operations  1.45 us (3%)
    pallas_call x1, Pallas kernels, fused(): pl.pallas_call(fused_kernel, out_shape=(jax.ShapeDtypeStruct((ROWS, SLAB,...  48.2 us
    pallas_call x1, Pallas kernels, outputs(): pl.pallas_call(output_kernel, out_shape=tuple((jax.ShapeDtypeStruct(s, F3...  7.41 us

profile of v1, /device:TPU:1, one launch (start us, length us, event | category | flops | bytes accessed | tf_op | source)
XLA Modules:
  0.0 57.0 jit_solution(15355813950621480226)
XLA Ops:
  1.3 48.2 %fused.1 = (bf16[32,8,2304]{2,1,0:T(8,128)(2,1)}, bf16[32,8,512]{2,1,0:T(8,128)(2,1)}, bf16[512,512]{1,0:T(8,128)(2,1)}, f32[256,256]{1,0:T(8,128)}, f32[8,128]{1,0:T(8,128)}, /*index=5*/f32[256,256]{1,0:T(8,128)}) custom-call(f32[1]{0:T(128)S(6)} %copy.7.ridge, bf16[8,1792]{1,0:T(8,128)(2,1)} %keys.1, bf16[8,512]{1,0:T(8,128)(2,1)} %shifts.1), custom_call_target="tpu_custom_call" | custom-call | tf_op jit(solution)/shard_map/fused/pallas_call | solution.py:412
  49.4 7.4 %outputs.1 = (f32[448,256]{1,0:T(8,128)}, f32[448,256]{1,0:T(8,128)}, f32[448,1792]{1,0:T(8,128)}, f32[448,512]{1,0:T(8,128)}) custom-call(bf16[512,512]{1,0:T(8,128)(2,1)} %get-tuple-element.10.q2_ref, f32[256,256]{1,0:T(8,128)} %get-tuple-element.11.m_ref, f32[8,128]{1,0:T(8,128)} %get-tuple-element.12.amount_ref, f32[256,256]{1,0:T(8,128)} %get-tuple-element.13.u_ref, ...), custom_call_target="tpu_custom_call" | custom-call | tf_op jit(solution)/shard_map/outputs/pallas_call | solution.py:520

commit v2 on v1

--- a/solution.py
+++ b/solution.py
@@ -114,15 +114,13 @@
 
 
 XS = COLS // 2
-A_LANES = pl.ds(0, 1152)
-B_LANES = pl.ds(1152, 1152)
-B_HALVES = (pl.ds(1152, 640), pl.ds(1792, 512))
+HALVES = (pl.ds(0, 1152), pl.ds(1152, 1152))
 
 
 def fused_kernel(
     ridge, keys, shifts, wide, window, q2_out, m_ref, amount_ref, u_out,
     crit, sums, own_sum, x_sums, R,
-    s_local, s_x, r_x, s_r, r_r, s_p, r_p, s_y, r_y, s_a, r_a, s_b, r_b, s_yb, r_yb, s_w, r_w, s_v, r_v,
+    s_local, s_x, r_x, s_r, r_r, s_p, r_p, s_own, r_own, s_z, r_z, s_y, r_y, s_w, r_w, s_v, r_v,
 ):
     row, col = lax.axis_index("row"), lax.axis_index("col")
     z, y = row // YS, lax.rem(row, YS)
@@ -181,6 +179,32 @@
         copy.wait()
     pl.semaphore_wait(barrier, ROWS + XS - 1)
 
+    up = lax.rem(z + 1, ZS) * YS
+    down = lax.rem(z + ZS - 1, ZS) * YS
+
+    def over_y(slot, send, recv):
+        for i in range(1, YS):
+            ref = wide.at[slot * YS + y]
+            remote(ref, ref, send, recv, z * YS + lax.rem(y + i, YS), col).start()
+
+    def step_ref(slot, step, way):
+        ref = wide.at[slot * YS + y]
+        return ref if step < 3 else ref.at[:, HALVES[way]]
+
+    def round_z(step):
+        for way, (source, target) in enumerate(((lax.rem(z + ZS - step, ZS), up), (lax.rem(z + step, ZS), down))):
+            ref = step_ref(source, step, way)
+            remote(ref, ref, s_z.at[way, step], r_z.at[way, step], target + y, col).start()
+
+    def wait_z(step, sems):
+        for way in range(2):
+            await_bytes(step_ref(0, step, way), sems.at[way, step])
+
+    def spread_y(step):
+        over_y(lax.rem(z + ZS - step - 1, ZS), s_y.at[0, step], r_y.at[0, step])
+        if step < 3:
+            over_y(lax.rem(z + step + 1, ZS), s_y.at[1, step], r_y.at[1, step])
+
     @pl.when(col < 2)
     def _():
         for i in range(1, XS):
@@ -191,6 +215,8 @@
     for i in range(1, XS):
         remote(own_sum.at[0], x_sums.at[x], s_x.at[1], r_x.at[1], row, lax.rem(col + 2 * i, COLS)).start()
     x_sums[x] = own_sum[0]
+    over_y(z, s_own, r_own)
+    round_z(0)
 
     @pl.when(col >= 2)
     def _():
@@ -208,52 +234,18 @@
     sums[core, row] = jnp.sum(x_sums[...], axis=0)
     lax.fori_loop(1, ROWS, send_slab, 0)
     lax.fori_loop(1, ROWS, send_sum, 0)
+    wait_z(0, r_z)
+    round_z(1)
     await_bytes(crit.at[0, pl.ds(0, ROWS - 1)], r_r.at[0])
     await_bytes(sums.at[0, pl.ds(0, ROWS - 1)], r_r.at[1])
 
     remote(crit.at[core], crit.at[core], s_p.at[0], r_p.at[0], row, partner).start()
     remote(sums.at[core], sums.at[core], s_p.at[1], r_p.at[1], row, partner).start()
 
-    up = lax.rem(z + 1, ZS) * YS
-    down = lax.rem(z + ZS - 1, ZS) * YS
-
-    def over_y(slot, lanes, send, recv):
-        for i in range(1, YS):
-            ref = wide.at[slot * YS + y, :, lanes]
-            remote(ref, ref, send, recv, z * YS + lax.rem(y + i, YS), col).start()
-
-    def round_b(step):
-        for way, (source, target) in enumerate(((lax.rem(z + ZS - step, ZS), up), (lax.rem(z + step, ZS), down))):
-            lanes = B_LANES if step < 3 else B_HALVES[way]
-            ref = wide.at[source * YS + y, :, lanes]
-            remote(ref, ref, s_b.at[way, step], r_b.at[way, step], target + y, col).start()
-
-    def wait_b(step, sems):
-        for way in range(2):
-            lanes = B_LANES if step < 3 else B_HALVES[way]
-            await_bytes(wide.at[0, :, lanes], sems.at[way, step])
-
-    def pairs_a(step, way):
-        return (0, 1) if step < 3 else (way,)
-
-    def round_a(step):
-        for pair in range(2):
-            for way, (source, target) in enumerate(((lax.rem(z + ZS - step, ZS), up), (lax.rem(z + step, ZS), down))):
-                if step > 0:
-                    await_bytes(wide.at[pl.ds(0, 2), :, A_LANES], r_a.at[way, step - 1, pair])
-                if pair in pairs_a(step, way):
-                    ref = wide.at[pl.ds(source * YS + 2 * pair, 2), :, A_LANES]
-                    remote(ref, ref, s_a.at[way, step, pair], r_a.at[way, step, pair], target + y, col).start()
-
-    def b_over_y(step):
-        if step < 3:
-            over_y(lax.rem(z + ZS - step - 1, ZS), B_LANES, s_yb.at[0, step], r_yb.at[0, step])
-            over_y(lax.rem(z + step + 1, ZS), B_LANES, s_yb.at[1, step], r_yb.at[1, step])
-        else:
-            over_y(lax.rem(z + ZS // 2, ZS), B_LANES, s_yb.at[0, step], r_yb.at[0, step])
-
-    over_y(z, pl.ds(0, WIDE), s_y, r_y)
-    round_b(0)
+    spread_y(0)
+    wait_z(1, r_z)
+    round_z(2)
+    spread_y(1)
 
     for yy in range(YS):
         start = yy * ROW_UNITS - 64 * (yy % 2)
@@ -277,31 +269,16 @@
 
             remote(window, window, s_v, r_v, row, partner).start()
 
-    def hook1():
-        await_bytes(wide.at[pl.ds(0, YS - 1)], r_y)
-        round_a(0)
-        wait_b(0, r_b)
-        round_b(1)
-        b_over_y(0)
-
-    def hook2():
-        round_a(1)
-        wait_b(1, r_b)
-        round_b(2)
-        b_over_y(1)
-
-    def hook3():
-        round_a(2)
-        wait_b(2, r_b)
-        round_b(3)
-        b_over_y(2)
-
-    def hook4():
-        round_a(3)
-        wait_b(3, r_b)
-        b_over_y(3)
-
-    hooks = {3: hook1, 9: hook2, 15: hook3, 21: hook4, 24: swap_window}
+    def hook_three():
+        wait_z(2, r_z)
+        round_z(3)
+        spread_y(2)
+
+    def hook_four():
+        wait_z(3, r_z)
+        spread_y(3)
+
+    hooks = {4: hook_three, 12: hook_four, 24: swap_window}
 
     await_bytes(crit.at[0], r_p.at[0])
     await_bytes(sums.at[0], r_p.at[1])
@@ -363,12 +340,10 @@
             copy.start()
             copy.wait()
 
-    for way in range(2):
-        for pair in pairs_a(3, way):
-            await_bytes(wide.at[pl.ds(0, 2), :, A_LANES], r_a.at[way, 3, pair])
+    await_bytes(wide.at[pl.ds(0, YS - 1)], r_own)
     for step in range(4):
         for way in range(2 if step < 3 else 1):
-            await_bytes(wide.at[pl.ds(0, YS - 1), :, B_LANES], r_yb.at[way, step])
+            await_bytes(wide.at[pl.ds(0, YS - 1)], r_y.at[way, step])
 
     @pl.when(core != lax.rem(z, 2))
     def _():
@@ -383,14 +358,11 @@
     await_bytes(sums.at[0, pl.ds(0, ROWS - 1)], s_r.at[1])
     await_bytes(crit.at[0], s_p.at[0])
     await_bytes(sums.at[0], s_p.at[1])
-    await_bytes(wide.at[pl.ds(0, YS - 1)], s_y)
+    await_bytes(wide.at[pl.ds(0, YS - 1)], s_own)
     for step in range(4):
-        wait_b(step, s_b)
-        for way in range(2):
-            for pair in pairs_a(step, way):
-                await_bytes(wide.at[pl.ds(0, 2), :, A_LANES], s_a.at[way, step, pair])
+        wait_z(step, s_z)
         for way in range(2 if step < 3 else 1):
-            await_bytes(wide.at[pl.ds(0, YS - 1), :, B_LANES], s_yb.at[way, step])
+            await_bytes(wide.at[pl.ds(0, YS - 1)], s_y.at[way, step])
 
     @pl.when(z == col)
     def _():
@@ -428,7 +400,7 @@
             pltpu.VMEM((XS, 1, 128), F32),
             pltpu.VMEM((2 * PANEL, 2 * PANEL + KEYS), F32),
             dma((3,)), dma((2,)), dma((2,)), dma((2,)), dma((2,)), dma((2,)), dma((2,)), dma, dma,
-            dma((2, 4, 2)), dma((2, 4, 2)), dma((2, 4)), dma((2, 4)), dma((2, 4)), dma((2, 4)),
+            dma((2, 4)), dma((2, 4)), dma((2, 4)), dma((2, 4)),
             dma, dma, dma, dma,
         ],
         compiler_params=pltpu.CompilerParams(collective_id=0, has_side_effects=True),
@@ -437,67 +409,47 @@
 
 
 def output_kernel(
-    q2_ref, m_ref, amount_ref, u_ref, win_ref, wide_ref, pa_out, pb_out, tr_out, fw_out,
-    kt, pa, pb, tr, fw, sems,
+    q2, m, amount_ref, u_hbm, win, wide, pa_out, pb_out, tr_out, fw_out,
+    u, kt, pa, pb, tr, fw, in_sem, sems,
 ):
     row, col = lax.axis_index("row"), lax.axis_index("col")
     z, y = row // YS, lax.rem(row, YS)
-    kt[...] = jnp.transpose(win_ref[...].astype(F32)).astype(BF16)
+    chunks = COL_UNITS // 256
+    special = (row == 0) | (row == YS)
+
+    load_u = pltpu.make_async_copy(u_hbm, u, in_sem)
+
+    @pl.when(special)
+    def _():
+        load_u.start()
+
+    kt[...] = jnp.transpose(win[...].astype(F32)).astype(BF16)
     off = pl.multiple_of(64 * lax.rem(y, 2), 64)
     k_rows = kt[pl.ds(off, ROW_UNITS), :]
-    q2 = q2_ref[...]
-    both = mm_nt(jnp.concatenate([k_rows, k_rows], axis=1), q2)
-    pa[...] = both[:, :PANEL]
-    pb[...] = both[:, PANEL:]
-    i0 = lax.broadcasted_iota(jnp.int32, (PANEL, PANEL), 0)
-    i1 = lax.broadcasted_iota(jnp.int32, (PANEL, PANEL), 1)
-
-    @pl.when(row == 0)
-    def _():
-        pa[:PANEL, :] = jnp.where(i0 >= i1, jnp.transpose(u_ref[...]), 0.0)
-        pb[:PANEL, :] = jnp.zeros((PANEL, PANEL), F32)
-
-    @pl.when(row == YS)
-    def _():
-        pb[:PANEL, :] = jnp.where(i0 >= i1, jnp.transpose(u_ref[...]), 0.0)
-
-    copies = [pltpu.make_async_copy(pa, pa_out, sems.at[0]), pltpu.make_async_copy(pb, pb_out, sems.at[1])]
-    for copy in copies:
-        copy.start()
-
-    mh, mm_, ml = split3(m_ref[...])
-    t = mm(jnp.concatenate([k_rows, k_rows, k_rows], axis=1), jnp.concatenate([mh, mm_, ml], axis=0))
-    th, tl = split2(t)
+    k_rows2 = jnp.concatenate([k_rows, k_rows], axis=1)
+    mh, ml = split2(m[...])
+    th, tl = split2(mm(k_rows2, jnp.concatenate([mh, ml], axis=0)))
     t2 = jnp.concatenate([th, tl], axis=1)
 
-    v = wide_ref[:, COL_UNITS:]
-    v2 = jnp.concatenate([v, v], axis=0)
-    fw[...] = mm(t2, v2)
-
-    @pl.when(row == 0)
-    def _():
-        fw[:PANEL, :] = mm(q2[:PANEL], v2)
-
-    @pl.when(row == YS)
-    def _():
-        fw[:PANEL, :] = mm(q2[PANEL:], v2)
-
-    copies.append(pltpu.make_async_copy(fw, fw_out, sems.at[2]))
-    copies[-1].start()
-
-    for q in range(COL_UNITS // 256):
+    copies = []
+
+    def send(src, dst, sem):
+        copies.append(pltpu.make_async_copy(src, dst, sems.at[sem]))
+        copies[-1].start()
+
+    def trailing_chunk(q):
         lanes = pl.ds(256 * q, 256)
-        k = wide_ref[:, 256 * q : 256 * q + 256]
+        k = wide[:, 256 * q : 256 * q + 256]
         tr[:, lanes] = mm(t2, jnp.concatenate([k, k], axis=0))
 
-        @pl.when(z == col)
+        @pl.when((z == col) & (y * ROW_UNITS < 256 * (q + 1)) & ((y + 1) * ROW_UNITS > 256 * q))
         def _():
             r0 = lax.broadcasted_iota(jnp.int32, (ROW_UNITS, 256), 0)
             r1 = lax.broadcasted_iota(jnp.int32, (ROW_UNITS, 256), 1)
             hit = r1 + (256 * q) == r0 + y * ROW_UNITS
             tr[:, lanes] += jnp.where(hit, amount_ref[0:1, 0:1], 0.0)
 
-        @pl.when((row == 0) | (row == YS))
+        @pl.when(special)
         def _():
             tr[:PANEL, lanes] = jnp.zeros((PANEL, 256), F32)
 
@@ -507,8 +459,43 @@
             def _():
                 tr[:, lanes] = jnp.zeros((ROW_UNITS, 256), F32)
 
-        copies.append(pltpu.make_async_copy(tr.at[:, lanes], tr_out.at[:, lanes], sems.at[3 + q]))
-        copies[-1].start()
+        send(tr.at[:, lanes], tr_out.at[:, lanes], 3 + q)
+
+    for q in range(3):
+        trailing_chunk(q)
+
+    both = mm_nt(k_rows2, q2[...])
+    pa[...] = both[:, :PANEL]
+    pb[...] = both[:, PANEL:]
+
+    @pl.when(special)
+    def _():
+        load_u.wait()
+        i0 = lax.broadcasted_iota(jnp.int32, (PANEL, PANEL), 0)
+        i1 = lax.broadcasted_iota(jnp.int32, (PANEL, PANEL), 1)
+        lower = jnp.where(i0 >= i1, jnp.transpose(u[...]), 0.0)
+        pb[:PANEL, :] = lower
+
+        @pl.when(row == 0)
+        def _():
+            pa[:PANEL, :] = lower
+            pb[:PANEL, :] = jnp.zeros((PANEL, PANEL), F32)
+
+    send(pa, pa_out, 0)
+    send(pb, pb_out, 1)
+
+    v = wide[:, COL_UNITS:]
+    v2 = jnp.concatenate([v, v], axis=0)
+    fw[...] = mm(t2, v2)
+
+    @pl.when(special)
+    def _():
+        start = pl.multiple_of(PANEL * (row // YS), PANEL)
+        fw[:PANEL, :] = mm(q2[pl.ds(start, PANEL), :], v2)
+
+    send(fw, fw_out, 2)
+    for q in range(3, chunks):
+        trailing_chunk(q)
     for copy in copies:
         copy.wait()
 
@@ -517,14 +504,18 @@
     vmem = pl.BlockSpec(memory_space=pltpu.VMEM)
     anyspace = pl.BlockSpec(memory_space=pl.ANY)
     shapes = [(ROW_UNITS, PANEL), (ROW_UNITS, PANEL), (ROW_UNITS, COL_UNITS), (ROW_UNITS, SHIFTS)]
+    chunks = COL_UNITS // 256
     return pl.pallas_call(
         output_kernel,
         out_shape=tuple(jax.ShapeDtypeStruct(s, F32) for s in shapes),
-        in_specs=[vmem] * 6,
+        in_specs=[vmem, vmem, vmem, anyspace, vmem, vmem],
         out_specs=(anyspace,) * 4,
-        scratch_shapes=[pltpu.VMEM((WIN, KEYS), BF16)]
+        scratch_shapes=[
+            pltpu.VMEM((PANEL, PANEL), F32),
+            pltpu.VMEM((WIN, KEYS), BF16),
+        ]
         + [pltpu.VMEM(s, F32) for s in shapes]
-        + [pltpu.SemaphoreType.DMA((3 + COL_UNITS // 256,))],
+        + [pltpu.SemaphoreType.DMA, pltpu.SemaphoreType.DMA((3 + chunks,))],
         name="outputs",
     )(q2, m, amount, u, win, wide)
 

time: 57.2 us -> 50.3 us (0.88)
  Pallas kernels: 55.6 us -> 48.7 us
    pallas_call x1, Pallas kernels: 48.2 us -> 41.6 us  [fused(): pl.pallas_call(fused_kernel, out_shape=(jax.ShapeDtypeStruct((ROWS, SLAB,...]
where the time goes in v2:
time: 50.3 us; the launch traced here: 50.1 us
  Pallas kernels  48.7 us (97%)
  between operations  1.45 us (3%)
    pallas_call x1, Pallas kernels, fused(): pl.pallas_call(fused_kernel, out_shape=(jax.ShapeDtypeStruct((ROWS, SLAB,...  41.6 us
    pallas_call x1, Pallas kernels, outputs(): pl.pallas_call(output_kernel, out_shape=tuple((jax.ShapeDtypeStruct(s, F3...  7.1 us

profile of v2, /device:TPU:1, one launch (start us, length us, event | category | flops | bytes accessed | tf_op | source)
XLA Modules:
  0.0 50.1 jit_solution(3899670646178970921)
XLA Ops:
  1.3 41.6 %fused.1 = (bf16[32,8,2304]{2,1,0:T(8,128)(2,1)}, bf16[32,8,512]{2,1,0:T(8,128)(2,1)}, bf16[512,512]{1,0:T(8,128)(2,1)}, f32[256,256]{1,0:T(8,128)}, f32[8,128]{1,0:T(8,128)}, /*index=5*/f32[256,256]{1,0:T(8,128)}) custom-call(f32[1]{0:T(128)S(6)} %copy.7.ridge, bf16[8,1792]{1,0:T(8,128)(2,1)} %keys.1, bf16[8,512]{1,0:T(8,128)(2,1)} %shifts.1), custom_call_target="tpu_custom_call" | custom-call | tf_op jit(solution)/shard_map/fused/pallas_call | solution.py:384
  42.9 7.1 %outputs.1 = (f32[448,256]{1,0:T(8,128)}, f32[448,256]{1,0:T(8,128)}, f32[448,1792]{1,0:T(8,128)}, f32[448,512]{1,0:T(8,128)}) custom-call(bf16[512,512]{1,0:T(8,128)(2,1)} %get-tuple-element.10.q2, f32[256,256]{1,0:T(8,128)} %get-tuple-element.11.m, f32[8,128]{1,0:T(8,128)} %get-tuple-element.12.amount_ref, f32[256,256]{1,0:T(8,128)} %get-tuple-element.13.u_hbm, ...), custom_call_target="tpu_custom_call" | custom-call | tf_op jit(solution)/shard_map/outputs/pallas_call | solution.py:508

commit v3 on v2

--- a/solution.py
+++ b/solution.py
@@ -52,7 +52,7 @@
     return jnp.broadcast_to(v[k : k + 1, :], (8, v.shape[1]))
 
 
-def factor16(R, base, s, j, nt, diag_next):
+def factor16(R, base, s, j, nt, diag_next, early):
     o = 16 * j
     iota = lax.broadcasted_iota(jnp.int32, (8, 128), 0)
     last = j == 7
@@ -64,7 +64,11 @@
     C = [[None] * 4 for _ in range(16)]
     for k in range(16):
         for g in range(k // 8, ng):
-            C[k][g] = jnp.broadcast_to(T[g][:, o + k : o + k + 1], (8, 128))
+            if early is not None and g == 0:
+                C[k][g] = early[k]
+            else:
+                C[k][g] = jnp.broadcast_to(T[g][:, o + k : o + k + 1], (8, 128))
+    ahead = None
     Y = {t: [R[base + 8 * g : base + 8 * g + 8, 128 * t : 128 * t + 128] for g in range(2)] for t in range(s + 1, nt)}
     rv = [jnp.zeros((8, 128), F32)] * 2
     for k in range(16):
@@ -89,13 +93,18 @@
             for g in range(gk, 2):
                 if M[g] is not None:
                     Y[t][g] = Y[t][g] - M[g] * yk
+        if not last:
+            if k == 11:
+                ahead = [jnp.broadcast_to(T[2][:, o + 16 + q : o + 17 + q], (8, 128)) for q in range(8)]
+            elif k > 11:
+                ahead = [ahead[q] - M[2] * row_bcast(C[k][2], q) for q in range(8)]
     U = {s: jnp.concatenate([T[0] * rv[0], T[1] * rv[1]], axis=0)}
     for t in range(s + 1, nt):
         U[t] = jnp.concatenate([Y[t][0] * rv[0], Y[t][1] * rv[1]], axis=0)
     for t in range(s, nt):
         R[base : base + 16, 128 * t : 128 * t + 128] = U[t]
     if last:
-        return None
+        return None, None
     zero = jnp.zeros((16, 128), BF16)
     parts = {t: split3(U[t]) for t in range(s, nt)}
     h, m, l = parts[s]
@@ -110,7 +119,7 @@
                 R[base + 32 : base + 16 + below, lanes] -= mm(left[16:], right)
         else:
             R[base + 16 : base + 16 + below, 128 * t : 128 * t + 128] -= mm(left, right)
-    return T[2], T[3]
+    return (T[2], T[3]), ahead
 
 
 XS = COLS // 2
@@ -278,7 +287,7 @@
         wait_z(3, r_z)
         spread_y(3)
 
-    hooks = {4: hook_three, 12: hook_four, 24: swap_window}
+    hooks = {7: hook_three, 15: hook_four, 23: swap_window}
 
     await_bytes(crit.at[0], r_p.at[0])
     await_bytes(sums.at[0], r_p.at[1])
@@ -307,9 +316,9 @@
     i1 = lax.broadcasted_iota(jnp.int32, (KEYS, KEYS), 1)
     m_ref[...] = jnp.where(i0 == i1, 1.0, 0.0).astype(F32)
     for s in range(nsuper):
-        following = None
+        following, early = None, None
         for j in range(8):
-            following = factor16(R, 128 * s + 16 * j, s, j, nt, following)
+            following, early = factor16(R, 128 * s + 16 * j, s, j, nt, following, early)
             if 8 * s + j in hooks:
                 hooks[8 * s + j]()
         us = R[128 * s : 128 * s + 128, 128 * s + 128 :]
@@ -427,8 +436,8 @@
     off = pl.multiple_of(64 * lax.rem(y, 2), 64)
     k_rows = kt[pl.ds(off, ROW_UNITS), :]
     k_rows2 = jnp.concatenate([k_rows, k_rows], axis=1)
-    mh, ml = split2(m[...])
-    th, tl = split2(mm(k_rows2, jnp.concatenate([mh, ml], axis=0)))
+    m_parts = jnp.concatenate(split3(m[...]), axis=0)
+    th, tl = split2(mm(jnp.concatenate([k_rows, k_rows, k_rows], axis=1), m_parts))
     t2 = jnp.concatenate([th, tl], axis=1)
 
     copies = []

time: 50.3 us -> 48.7 us (0.968)
  Pallas kernels: 48.7 us -> 47.1 us
    pallas_call x1, Pallas kernels: 41.6 us -> 39.9 us  [fused(): pl.pallas_call(fused_kernel, out_shape=(jax.ShapeDtypeStruct((ROWS, SLAB,...]
where the time goes in v3:
time: 48.7 us; the launch traced here: 48.5 us
  Pallas kernels  47.1 us (97%)
  between operations  1.45 us (3%)
    pallas_call x1, Pallas kernels, fused(): pl.pallas_call(fused_kernel, out_shape=(jax.ShapeDtypeStruct((ROWS, SLAB,...  39.9 us
    pallas_call x1, Pallas kernels, outputs(): pl.pallas_call(output_kernel, out_shape=tuple((jax.ShapeDtypeStruct(s, F3...  7.18 us

profile of v3, /device:TPU:1, one launch (start us, length us, event | category | flops | bytes accessed | tf_op | source)
XLA Modules:
  0.0 48.5 jit_solution(7489459027985906880)
XLA Ops:
  1.3 39.9 %fused.1 = (bf16[32,8,2304]{2,1,0:T(8,128)(2,1)}, bf16[32,8,512]{2,1,0:T(8,128)(2,1)}, bf16[512,512]{1,0:T(8,128)(2,1)}, f32[256,256]{1,0:T(8,128)}, f32[8,128]{1,0:T(8,128)}, /*index=5*/f32[256,256]{1,0:T(8,128)}) custom-call(f32[1]{0:T(128)S(6)} %copy.7.ridge, bf16[8,1792]{1,0:T(8,128)(2,1)} %keys.1, bf16[8,512]{1,0:T(8,128)(2,1)} %shifts.1), custom_call_target="tpu_custom_call" | custom-call | tf_op jit(solution)/shard_map/fused/pallas_call | solution.py:393
  41.2 7.2 %outputs.1 = (f32[448,256]{1,0:T(8,128)}, f32[448,256]{1,0:T(8,128)}, f32[448,1792]{1,0:T(8,128)}, f32[448,512]{1,0:T(8,128)}) custom-call(bf16[512,512]{1,0:T(8,128)(2,1)} %get-tuple-element.10.q2, f32[256,256]{1,0:T(8,128)} %get-tuple-element.11.m, f32[8,128]{1,0:T(8,128)} %get-tuple-element.12.amount_ref, f32[256,256]{1,0:T(8,128)} %get-tuple-element.13.u_hbm, ...), custom_call_target="tpu_custom_call" | custom-call | tf_op jit(solution)/shard_map/outputs/pallas_call | solution.py:517

commit v4 on v3

--- a/solution.py
+++ b/solution.py
@@ -151,7 +151,7 @@
     for i in range(1, XS):
         greet(row, lax.rem(col + 2 * i, COLS))
     greet(row, partner)
-    lax.fori_loop(1, ROWS, greet_row, 0)
+    lax.fori_loop(1, ROWS, greet_row, 0, unroll=True)
 
     k32 = keys[...].astype(F32)
     sq = k32 * k32
@@ -241,8 +241,8 @@
 
     await_bytes(x_sums.at[pl.ds(0, XS - 1)], r_x.at[1])
     sums[core, row] = jnp.sum(x_sums[...], axis=0)
-    lax.fori_loop(1, ROWS, send_slab, 0)
-    lax.fori_loop(1, ROWS, send_sum, 0)
+    lax.fori_loop(1, ROWS, send_slab, 0, unroll=True)
+    lax.fori_loop(1, ROWS, send_sum, 0, unroll=True)
     wait_z(0, r_z)
     round_z(1)
     await_bytes(crit.at[0, pl.ds(0, ROWS - 1)], r_r.at[0])
@@ -259,11 +259,14 @@
     for yy in range(YS):
         start = yy * ROW_UNITS - 64 * (yy % 2)
         target = col * YS + yy
-        for i in range(XS):
-
-            @pl.when((target != row) | (i != x))
-            def _():
-                remote(keys.at[:, pl.ds(start, WIN)], window.at[row], s_w, r_w, target, 2 * i + core).start()
+        for i in range(1, XS):
+            remote(
+                keys.at[:, pl.ds(start, WIN)], window.at[row], s_w, r_w, target, lax.rem(col + 2 * i, COLS)
+            ).start()
+
+        @pl.when(target != row)
+        def _():
+            remote(keys.at[:, pl.ds(start, WIN)], window.at[row], s_w, r_w, target, col).start()
 
     def swap_window():
         @pl.when(core == lax.rem(z, 2))

time: 48.7 us -> 48.3 us (level)
  no operation moved by 1% of the time
where the time goes in v4:
time: 48.3 us; the launch traced here: 48.2 us
  Pallas kernels  46.9 us (97%)
  between operations  1.29 us (3%)
    pallas_call x1, Pallas kernels, fused(): pl.pallas_call(fused_kernel, out_shape=(jax.ShapeDtypeStruct((ROWS, SLAB,...  39.9 us
    pallas_call x1, Pallas kernels, outputs(): pl.pallas_call(output_kernel, out_shape=tuple((jax.ShapeDtypeStruct(s, F3...  7.02 us

profile of v4, /device:TPU:1, one launch (start us, length us, event | category | flops | bytes accessed | tf_op | source)
XLA Modules:
  0.0 48.2 jit_solution(15624650787556550342)
XLA Ops:
  1.3 39.9 %fused.1 = (bf16[32,8,2304]{2,1,0:T(8,128)(2,1)}, bf16[32,8,512]{2,1,0:T(8,128)(2,1)}, bf16[512,512]{1,0:T(8,128)(2,1)}, f32[256,256]{1,0:T(8,128)}, f32[8,128]{1,0:T(8,128)}, /*index=5*/f32[256,256]{1,0:T(8,128)}) custom-call(f32[1]{0:T(128)S(6)} %copy.7.ridge, bf16[8,1792]{1,0:T(8,128)(2,1)} %keys.1, bf16[8,512]{1,0:T(8,128)(2,1)} %shifts.1), custom_call_target="tpu_custom_call" | custom-call | tf_op jit(solution)/shard_map/fused/pallas_call | solution.py:396
  41.1 7.0 %outputs.1 = (f32[448,256]{1,0:T(8,128)}, f32[448,256]{1,0:T(8,128)}, f32[448,1792]{1,0:T(8,128)}, f32[448,512]{1,0:T(8,128)}) custom-call(bf16[512,512]{1,0:T(8,128)(2,1)} %get-tuple-element.10.q2, f32[256,256]{1,0:T(8,128)} %get-tuple-element.11.m, f32[8,128]{1,0:T(8,128)} %get-tuple-element.12.amount_ref, f32[256,256]{1,0:T(8,128)} %get-tuple-element.13.u_hbm, ...), custom_call_target="tpu_custom_call" | custom-call | tf_op jit(solution)/shard_map/outputs/pallas_call | solution.py:520
